TPU v7x, 256 devices: a whole 4x4x8 slice. The times are simulated.
256 devices in a mesh: band: 64 (over z, y_hi, x), mem: 4 (over y_lo, core).
Axes of the slice: x: 4, y: 4 (y_hi: 2, y_lo: 2; y = y_hi * 2 + y_lo), z: 8, core: 2. Of those that a mesh axis runs over, the one named last changes fastest.
Arguments:
- coef: float32 [2, 512, 128, 2, 512], P(None, 'band', 'mem'), may hold values from -6 to 6
- perturb: bfloat16 [768, 128, 2, 1536], P('band', 'mem'), may hold values from -6 to 6
- weight: float32 [768, 2, 1536], P('band'), may hold values from 1 to 10
- table: bfloat16 [512, 512, 768], P('band'), may hold values from -0.0078125 to 0.0078125
- wave_map: int32 [512], replicated, may hold values from 0 to 511, each once
- lat_map: int32 [768], replicated, may hold values from 0 to 767, each once
Outputs:
- increment: float32 [768, 2, 1536], P('band')
- product: float32 [2, 512, 128, 2, 512], P(None, 'band', 'mem')
Inputs may be any that keep to these rules, and one draw needn't show every extreme that they name: A permutation: spectral row r holds zonal wavenumber wave_map[r]. A permutation: grid row s holds Gaussian latitude lat_map[s]; the last dimension of table stands in natural latitude order.
All inputs are finite; a program needn't handle non-finite values.
Results may differ from a plain program's by a relative error of at most 0.0048.
Values may be sent and summed in bfloat16 or wider, within the bound.
A program may use at most 128 MiB of HBM per device.

v0:
```python
import functools
import math

import jax
import jax.numpy as jnp
from jax import lax
from jax.experimental import pallas as pl
from jax.experimental.pallas import tpu as pltpu
from jax.sharding import PartitionSpec as P

MESH = pl.DeviceIdType.MESH
F32 = jnp.float32
BF16 = jnp.bfloat16

NCH = 3


def body_a(
    wave_ref, lat_ref, coef_hbm, pert_hbm, w_hbm, table_hbm,
    inc_out, back_out,
    tab_v, coef_v, pert_v, w_v, spec32, nat, send_f, recv_f, xt, dft, pert32, w8, part, recv_i, inc_v, adj, send_b,
    in_sem, tab_sem, fs_sem, fr_sem, is_sem, ir_sem, bs_sem, br_sem, loc_sem, out_sem,
):
    band = lax.axis_index("band")
    mem = lax.axis_index("mem")
    nb, nm = 64, 4
    nwave, nlat, lon = 512, 768, 1536

    tcopies = [
        pltpu.make_async_copy(table_hbm.at[r], tab_v.at[r], tab_sem.at[r]) for r in range(8)
    ]
    c_copy = pltpu.make_async_copy(coef_hbm, coef_v, in_sem.at[0])
    p_copy = pltpu.make_async_copy(pert_hbm, pert_v, in_sem.at[1])
    w_copy = pltpu.make_async_copy(w_hbm, w_v, in_sem.at[2])
    c_copy.start()
    for t in tcopies:
        t.start()
    p_copy.start()
    w_copy.start()

    barrier = pltpu.get_barrier_semaphore()

    def greet(i, c):
        pl.semaphore_signal(
            barrier, inc=1, device_id=(lax.rem(band + i, nb), mem), device_id_type=MESH
        )
        return c

    lax.fori_loop(1, nb, greet, 0)
    for i in range(1, nm):
        pl.semaphore_signal(
            barrier, inc=1, device_id=(band, lax.rem(mem + i, nm)), device_id_type=MESH
        )

    z, y, x = band // 8, lax.rem(band // 4, 2), lax.rem(band, 4)

    def peer(i):
        a, b = lax.rem(i, 8), 7 - i // 8
        dz = jnp.where(lax.rem(a, 2) == 0, 4 - a // 2, 5 + a // 2)
        dz = jnp.where(a == 7, 0, dz)
        dy, dx = b // 4, lax.rem(b, 4)
        return (lax.rem(z + dz, 8) * 2 + lax.rem(y + dy, 2)) * 4 + lax.rem(x + dx, 4)

    c_copy.wait()
    lane_j = lax.broadcasted_iota(jnp.int32, (2, nwave), 1)

    def to_spec(r, c):
        limit = nwave - wave_ref[band * 8 + r]
        keep = lane_j < limit
        for part_i in range(2):
            for k in range(32):
                v = coef_v[part_i, r, k]
                spec32[r, pl.ds(part_i * 64 + 2 * k, 2), :] = jnp.where(keep, v, 0.0)
        return c

    lax.fori_loop(0, 8, to_spec, 0)

    for r in range(8):
        tcopies[r].wait()
        f = jnp.dot(spec32[r].astype(BF16), tab_v[r], preferred_element_type=F32)
        nat.reshape(nlat * 8, 128)[pl.ds(r, nlat, stride=8), :] = f.T

    pl.semaphore_wait(barrier, nb - 1 + nm - 1)

    lane = lax.broadcasted_iota(jnp.int32, (8, 128), 1)
    left = lane < 64

    def send_chunk(buf, ch, dst, s_sem, r_sem):
        def one(i, c):
            e = peer(i)
            pltpu.make_async_remote_copy(
                buf.at[ch, e], dst.at[ch, band], s_sem.at[ch], r_sem.at[ch],
                device_id=(e, mem), device_id_type=MESH,
            ).start()
            return c

        lax.fori_loop(0, nb - 1, one, 0)

    def rest(buf, ch, dst, s_sem, r_sem):
        return pltpu.make_async_remote_copy(
            buf.at[ch, pl.ds(0, nb - 1)], dst.at[ch, pl.ds(0, nb - 1)], s_sem.at[ch], r_sem.at[ch],
            device_id=(lax.rem(band + 1, nb), mem), device_id_type=MESH,
        )

    def row(s):
        return nat[lat_ref[s]]

    for ch in range(NCH):

        def build(e, c):
            for p in range(2):
                s0 = e * 12 + ch * 4 + 2 * p
                a, b = row(s0), row(s0 + 1)
                lo = jnp.where(left, a, pltpu.roll(b, 64, 1))
                hi = jnp.where(left, pltpu.roll(a, 64, 1), b)
                send_f[ch, e, :, p * 128 : (p + 1) * 128] = jnp.concatenate(
                    [lo, hi], axis=0
                ).astype(BF16)
            return c

        lax.fori_loop(0, nb, build, 0)
        pltpu.make_async_copy(send_f.at[ch, band], recv_f.at[ch, band], loc_sem.at[ch]).start()
        send_chunk(send_f, ch, recv_f, fs_sem, fr_sem)

    row8 = lax.broadcasted_iota(jnp.int32, (8, 128), 0)

    def fourier(d, c):
        m = jnp.zeros((8, 128), jnp.int32)
        for i in range(8):
            m = jnp.where(row8 == i, wave_ref[d * 8 + i], m)
        low = lax.rem(m * lane, lon).astype(F32) * (2.0 * math.pi / lon)
        high = (lax.rem(m * lane, 12) * 128).astype(F32) * (2.0 * math.pi / lon)
        cb, sb = jnp.cos(low), jnp.sin(low)
        f = jnp.where(m == 0, 1.0, 2.0)
        fc, fs = f * jnp.cos(high), f * jnp.sin(high)
        for xb in range(12):
            ca = jnp.broadcast_to(fc[:, xb : xb + 1], (8, 128))
            sa = jnp.broadcast_to(fs[:, xb : xb + 1], (8, 128))
            dft[pl.ds(pl.multiple_of(d * 16, 16), 16), xb * 128 : (xb + 1) * 128] = (
                jnp.concatenate([ca * cb - sa * sb, -(sa * cb + ca * sb)], axis=0).astype(BF16)
            )
        return c

    lax.fori_loop(0, nb, fourier, 0)

    p_copy.wait()
    w_copy.wait()

    def to_rows(s, c):
        for k in range(32):
            pert32[s, pl.ds(2 * k, 2), :] = pert_v[s, k].astype(F32)
        return c

    lax.fori_loop(0, 12, to_rows, 0)
    for s in range(12):
        w8[s // 4, pl.ds(2 * (s % 4), 2), :] = w_v[s]

    scale = 1.0 / math.sqrt(32 * nm - 1)
    xw = 512

    for ch in range(NCH):
        pltpu.make_async_copy(send_f.at[ch, band], recv_f.at[ch, band], loc_sem.at[ch]).wait()
        rest(send_f, ch, recv_f, fs_sem, fr_sem).wait_recv()
        xt[...] = recv_f[ch].reshape(1024, 256).T

        def forward(i, c):
            cols = pl.ds(pl.multiple_of(i * xw, xw), xw)
            g = jnp.dot(xt[...], dft[:, cols], preferred_element_type=F32)
            for s in range(4):
                t = pert32[ch * 4 + s, :, cols] * g[s * 64 : (s + 1) * 64]
                t = jnp.sum(t.reshape(8, 8, xw), axis=0)
                t = t + pltpu.roll(t, 4, 0)
                t = t + pltpu.roll(t, 6, 0)
                part[ch, pl.ds(2 * s, 2), cols] = t[0:2]
            return c

        lax.fori_loop(0, lon // xw, forward, 0)

        copies = [
            pltpu.make_async_remote_copy(
                part.at[ch], recv_i.at[ch, i - 1], is_sem.at[ch, i - 1], ir_sem.at[ch, i - 1],
                device_id=(band, lax.rem(mem + i, nm)), device_id_type=MESH,
            )
            for i in range(1, nm)
        ]
        for cp in copies:
            cp.start()
        for cp in copies:
            cp.wait_recv()
        g0, g1, g2, g3 = part[ch], recv_i[ch, 0], recv_i[ch, 1], recv_i[ch, 2]
        inc = ((g0 + g2) + (g1 + g3)) * scale
        inc_v[pl.ds(8 * ch, 8), :] = inc
        w8[ch] = w8[ch] * inc * scale

        def backward(s):
            g = w8[ch, 2 * s : 2 * s + 2, :]
            g = jnp.concatenate([g] * 4, axis=0)
            a = pert32[ch * 4 + s].reshape(8, 8, lon) * g[None]
            adj[s * 64 : (s + 1) * 64, :] = a.reshape(64, lon).astype(BF16)

        for s in range(4):
            backward(s)

        def back(i, c):
            rows = pl.ds(pl.multiple_of(i * 256, 256), 256)
            v = lax.dot_general(
                dft[rows, :], adj[...], (((1,), (1,)), ((), ())), preferred_element_type=F32
            )
            send_b[ch, pl.ds(pl.multiple_of(i * 16, 16), 16)] = v.astype(BF16).reshape(16, 16, 256)
            return c

        lax.fori_loop(0, 4, back, 0)
        pltpu.make_async_copy(
            send_b.at[ch, band], back_out.at[ch, band], loc_sem.at[NCH + ch]
        ).start()
        send_chunk(send_b, ch, back_out, bs_sem, br_sem)

    for s in range(12):
        inc_out[s] = inc_v[pl.ds(2 * s, 2), :]

    for ch in range(NCH):
        rest(send_f, ch, recv_f, fs_sem, fr_sem).wait_send()
        for i in range(1, nm):
            pltpu.make_async_remote_copy(
                part.at[ch], recv_i.at[ch, i - 1], is_sem.at[ch, i - 1], ir_sem.at[ch, i - 1],
                device_id=(band, lax.rem(mem + i, nm)), device_id_type=MESH,
            ).wait_send()
        pltpu.make_async_copy(
            send_b.at[ch, band], back_out.at[ch, band], loc_sem.at[NCH + ch]
        ).wait()
        rest(send_b, ch, back_out, bs_sem, br_sem).wait()


def body_b(wave_ref, lat_ref, back_ref, table_ref, coef_ref, out_ref, nat, acc):
    r = pl.program_id(0)
    nlat, nwave = 768, 512
    lane = lax.broadcasted_iota(jnp.int32, (8, 128), 1)
    left = lane < 64

    @pl.when(r == 0)
    def _():
        def put(s, v):
            nat[pl.ds(pl.multiple_of(lat_ref[s] * 8, 8), 8), :] = v

        for ch in range(NCH):

            def open_up(e, c):
                for p in range(2):
                    s0 = e * 12 + ch * 4 + 2 * p
                    t = back_ref[ch, e, :, p * 128 : (p + 1) * 128].astype(F32)
                    lo, hi = t[0:8], t[8:16]
                    put(s0, jnp.where(left, lo, pltpu.roll(hi, 64, 1)))
                    put(s0 + 1, jnp.where(left, pltpu.roll(lo, 64, 1), hi))
                return c

            lax.fori_loop(0, 64, open_up, 0)

    a = nat[pl.ds(r, nlat, stride=8), :].astype(BF16)
    back = lax.dot_general(
        a, table_ref[0], (((0,), (1,)), ((), ())), preferred_element_type=F32
    )
    acc[...] = back
    keep = lax.broadcasted_iota(jnp.int32, (2, nwave), 1) < nwave - wave_ref[r]
    for c in range(2):
        for k in range(32):
            out_ref[c, 0, k] = jnp.where(
                keep, coef_ref[c, 0, k] + acc[pl.ds(c * 64 + 2 * k, 2), :], 0.0
            )


def body(coef, perturb, weight, table, wave_map, lat_map):
    any_ = pl.BlockSpec(memory_space=pl.ANY)
    smem = pl.BlockSpec(memory_space=pltpu.SMEM)
    dma = pltpu.SemaphoreType.DMA
    inc, back = pl.pallas_call(
        body_a,
        out_shape=(
            jax.ShapeDtypeStruct((12, 2, 1536), F32),
            jax.ShapeDtypeStruct((NCH, 64, 16, 256), BF16),
        ),
        in_specs=[smem, smem, any_, any_, any_, any_],
        out_specs=(pl.BlockSpec(memory_space=pltpu.VMEM), any_),
        scratch_shapes=[
            pltpu.VMEM((8, 512, 768), BF16),
            pltpu.VMEM((2, 8, 32, 2, 512), F32),
            pltpu.VMEM((12, 32, 2, 1536), BF16),
            pltpu.VMEM((12, 2, 1536), F32),
            pltpu.VMEM((8, 128, 512), F32),
            pltpu.VMEM((768, 8, 128), F32),
            pltpu.VMEM((NCH, 64, 16, 256), BF16),
            pltpu.VMEM((NCH, 64, 16, 256), BF16),
            pltpu.VMEM((256, 1024), BF16),
            pltpu.VMEM((1024, 1536), BF16),
            pltpu.VMEM((12, 64, 1536), F32),
            pltpu.VMEM((NCH, 8, 1536), F32),
            pltpu.VMEM((NCH, 8, 1536), F32),
            pltpu.VMEM((NCH, 3, 8, 1536), F32),
            pltpu.VMEM((24, 1536), F32),
            pltpu.VMEM((256, 1536), BF16),
            pltpu.VMEM((NCH, 64, 16, 256), BF16),
            dma((3,)),
            dma((8,)),
            dma((NCH,)),
            dma((NCH,)),
            dma((NCH, 3)),
            dma((NCH, 3)),
            dma((NCH,)),
            dma((NCH,)),
            dma((2 * NCH,)),
            dma,
        ],
        compiler_params=pltpu.CompilerParams(
            collective_id=0, has_side_effects=True, vmem_limit_bytes=60 * 1024 * 1024
        ),
        name="transforms",
    )(wave_map, lat_map, coef, perturb, weight, table)
    own = lax.dynamic_slice_in_dim(wave_map, lax.axis_index("band") * 8, 8)
    product = pl.pallas_call(
        body_b,
        out_shape=jax.ShapeDtypeStruct((2, 8, 32, 2, 512), F32),
        grid=(8,),
        in_specs=[
            smem,
            smem,
            pl.BlockSpec((NCH, 64, 16, 256), lambda r: (0, 0, 0, 0)),
            pl.BlockSpec((1, 512, 768), lambda r: (r, 0, 0)),
            pl.BlockSpec((2, 1, 32, 2, 512), lambda r: (0, r, 0, 0, 0)),
        ],
        out_specs=pl.BlockSpec((2, 1, 32, 2, 512), lambda r: (0, r, 0, 0, 0)),
        scratch_shapes=[pltpu.VMEM((768 * 8, 128), F32), pltpu.VMEM((128, 512), F32)],
        compiler_params=pltpu.CompilerParams(vmem_limit_bytes=60 * 1024 * 1024),
        name="product",
    )(own, lat_map, back, table, coef)
    return inc, product


def solution(mesh):
    in_specs = (
        P(None, "band", "mem", None, None),
        P("band", "mem", None, None),
        P("band", None, None),
        P("band", None, None),
        P(),
        P(),
    )
    out_specs = (P("band", None, None), P(None, "band", "mem", None, None))
    return jax.shard_map(body, mesh=mesh, in_specs=in_specs, out_specs=out_specs, check_vma=False)
```

profile of v0, /device:TPU:1, one launch (start us, length us, event | category | flops | bytes accessed | tf_op | source)
XLA Modules:
  0.0 121.0 jit_solution(9487854105789118460)
XLA Ops:
  0.6 1.3 %dynamic_slice.3.wave_ref = s32[8]{0:T(128)} dynamic-slice(s32[512]{0:T(512)} %wave_ref.1, s32[]{:T(128)S(6)} %select_n.3), dynamic_slice_sizes={8} | dynamic-slice | bytes 68 | tf_op jit(solution)/shard_map/dynamic_slice | solution.py:317
  1.9 94.5 %transforms.1 = (f32[12,2,1536]{2,1,0:T(2,128)}, bf16[3,64,16,256]{3,2,1,0:T(8,128)(2,1)}) custom-call(s32[512]{0:T(512)} %wave_ref.1, s32[768]{0:T(1024)} %lat_ref.3, f32[2,8,32,2,512]{4,3,2,1,0:T(2,128)} %coef_ref.1, bf16[12,32,2,1536]{3,2,1,0:T(2,128)(2,1)} %pert_hbm.1, f32[12,2,1536]{2,1,0:T(2,128)} %w_hbm.1, bf16[8,512,768]{2,1,0:T(8,128)(2,1)} %table_ref.1), custom_call_target="tpu_custom_call" | custom-call | tf_op jit(solution)/shard_map/transforms/pallas_call | solution.py:275
  96.4 0.0 copy-start
  96.4 23.9 %product.1 = f32[2,8,32,2,512]{4,3,2,1,0:T(2,128)} custom-call(s32[8]{0:T(128)} %dynamic_slice.3.wave_ref, s32[768]{0:T(1024)} %lat_ref.3, bf16[3,64,16,256]{3,2,1,0:T(8,128)(2,1)} %get-tuple-element.5.back_ref, bf16[8,512,768]{2,1,0:T(8,128)(2,1)} %table_ref.1, f32[2,8,32,2,512]{4,3,2,1,0:T(2,128)} %coef_ref.1), custom_call_target="tpu_custom_call" | custom-call | tf_op jit(solution)/shard_map/product/pallas_call | solution.py:318
  120.4 0.0 copy-done
  120.4 0.7 copy.9
Async XLA Ops:
  96.4 24.0 %copy-start = (f32[12,2,1536]{2,1,0:T(2,128)S(1)}, f32[12,2,1536]{2,1,0:T(2,128)}, u32[]{:S(2)}) copy-start(f32[12,2,1536]{2,1,0:T(2,128)} %get-tuple-element.8) | copy-start | bytes 442372
where the time goes:
time: 121 us
  Pallas kernels  118 us (98%)
  local copies, waits for them, and re-layouts  1.93 us (2%)
    pallas_call x1, Pallas kernels, body(): pl.pallas_call(body_a, out_shape=(jax.ShapeDtypeStruct((12, 2, 1536), F32...  94.5 us
    pallas_call x1, Pallas kernels, body(): pl.pallas_call(body_b, out_shape=jax.ShapeDtypeStruct((2, 8, 32, 2, 512),...  23.9 us

commit v1 on v0

--- a/solution.py
+++ b/solution.py
@@ -17,9 +17,9 @@
 
 def body_a(
     wave_ref, lat_ref, coef_hbm, pert_hbm, w_hbm, table_hbm,
-    inc_out, back_out,
+    inc_out, prod_out,
     tab_v, coef_v, pert_v, w_v, spec32, nat, send_f, recv_f, xt, dft, pert32, w8, part, recv_i, inc_v, adj, send_b,
-    in_sem, tab_sem, fs_sem, fr_sem, is_sem, ir_sem, bs_sem, br_sem, loc_sem, out_sem,
+    recv_b, pick, opened, in_sem, tab_sem, fs_sem, fr_sem, is_sem, ir_sem, bs_sem, br_sem, loc_sem, out_sem,
 ):
     band = lax.axis_index("band")
     mem = lax.axis_index("mem")
@@ -107,7 +107,8 @@
 
     for ch in range(NCH):
 
-        def build(e, c):
+        def build(i):
+            e = peer(i)
             for p in range(2):
                 s0 = e * 12 + ch * 4 + 2 * p
                 a, b = row(s0), row(s0 + 1)
@@ -116,11 +117,27 @@
                 send_f[ch, e, :, p * 128 : (p + 1) * 128] = jnp.concatenate(
                     [lo, hi], axis=0
                 ).astype(BF16)
-            return c
-
-        lax.fori_loop(0, nb, build, 0)
+
+        def send(i):
+            e = peer(i)
+            pltpu.make_async_remote_copy(
+                send_f.at[ch, e], recv_f.at[ch, band], fs_sem.at[ch], fr_sem.at[ch],
+                device_id=(e, mem), device_id_type=MESH,
+            ).start()
+
+        def step(g, c):
+            for k in range(4):
+                build(4 * g + k)
+            for k in range(4):
+                send(4 * g - 4 + k)
+            return c
+
+        for k in range(4):
+            build(k)
+        lax.fori_loop(1, nb // 4, step, 0)
+        for k in range(3):
+            send(nb - 4 + k)
         pltpu.make_async_copy(send_f.at[ch, band], recv_f.at[ch, band], loc_sem.at[ch]).start()
-        send_chunk(send_f, ch, recv_f, fs_sem, fr_sem)
 
     row8 = lax.broadcasted_iota(jnp.int32, (8, 128), 0)
 
@@ -141,7 +158,7 @@
             )
         return c
 
-    lax.fori_loop(0, nb, fourier, 0)
+    lax.fori_loop(0, nb, fourier, 0, unroll=2)
 
     p_copy.wait()
     w_copy.wait()
@@ -211,12 +228,69 @@
 
         lax.fori_loop(0, 4, back, 0)
         pltpu.make_async_copy(
-            send_b.at[ch, band], back_out.at[ch, band], loc_sem.at[NCH + ch]
+            send_b.at[ch, band], recv_b.at[ch, band], loc_sem.at[NCH + ch]
         ).start()
-        send_chunk(send_b, ch, back_out, bs_sem, br_sem)
+        send_chunk(send_b, ch, recv_b, bs_sem, br_sem)
 
     for s in range(12):
         inc_out[s] = inc_v[pl.ds(2 * s, 2), :]
+
+    def select(t, c):
+        halves = []
+        for h in range(2):
+            m = jnp.zeros((8, 128), jnp.int32)
+            for i in range(8):
+                k = h * 8 + i
+                m = jnp.where(row8 == i, lat_ref[(t % 16 * 4 + k // 4) * 12 + t // 16 * 4 + k % 4], m)
+            halves.append(m)
+        m = jnp.concatenate(halves, axis=0)
+        lane16 = lax.broadcasted_iota(jnp.int32, (16, 128), 1)
+        for b in range(nlat // 128):
+            pick[pl.ds(pl.multiple_of(t * 16, 16), 16), b * 128 : (b + 1) * 128] = jnp.where(
+                m == lane16 + b * 128, 1.0, 0.0
+            ).astype(BF16)
+        return c
+
+    lax.fori_loop(0, nlat // 16, select, 0, unroll=2)
+
+    def arrange(r, c):
+        tab_v[r] = lax.dot_general(
+            tab_v[r], pick[...], (((1,), (1,)), ((), ())), preferred_element_type=F32
+        ).astype(BF16)
+        return c
+
+    lax.fori_loop(0, 8, arrange, 0)
+
+    for ch in range(NCH):
+        pltpu.make_async_copy(
+            send_b.at[ch, band], recv_b.at[ch, band], loc_sem.at[NCH + ch]
+        ).wait()
+        rest(send_b, ch, recv_b, bs_sem, br_sem).wait_recv()
+
+        def open_up(g, c):
+            for k in range(8):
+                e = g * 8 + k
+                for p in range(2):
+                    t = recv_b[ch, e, :, p * 128 : (p + 1) * 128].astype(F32)
+                    lo, hi = t[0:8], t[8:16]
+                    opened[e * 4 + 2 * p] = jnp.where(left, lo, pltpu.roll(hi, 64, 1))
+                    opened[e * 4 + 2 * p + 1] = jnp.where(left, pltpu.roll(lo, 64, 1), hi)
+            return c
+
+        lax.fori_loop(0, nb // 8, open_up, 0)
+
+        for r in range(8):
+            a = opened.reshape(2048, 128)[pl.ds(r, 256, stride=8), :].astype(BF16)
+            v = lax.dot_general(
+                a, tab_v[r, :, ch * 256 : (ch + 1) * 256], (((0,), (1,)), ((), ())),
+                preferred_element_type=F32,
+            )
+            if ch < NCH - 1:
+                spec32[r] += v
+            else:
+                keep = lax.broadcasted_iota(jnp.int32, (128, nwave), 1) < nwave - wave_ref[band * 8 + r]
+                spec32[r] = jnp.where(keep, spec32[r] + v, 0.0)
+                pltpu.make_async_copy(spec32.at[r], prod_out.at[r], out_sem.at[r]).start()
 
     for ch in range(NCH):
         rest(send_f, ch, recv_f, fs_sem, fr_sem).wait_send()
@@ -225,61 +299,36 @@
                 part.at[ch], recv_i.at[ch, i - 1], is_sem.at[ch, i - 1], ir_sem.at[ch, i - 1],
                 device_id=(band, lax.rem(mem + i, nm)), device_id_type=MESH,
             ).wait_send()
-        pltpu.make_async_copy(
-            send_b.at[ch, band], back_out.at[ch, band], loc_sem.at[NCH + ch]
-        ).wait()
-        rest(send_b, ch, back_out, bs_sem, br_sem).wait()
-
-
-def body_b(wave_ref, lat_ref, back_ref, table_ref, coef_ref, out_ref, nat, acc):
-    r = pl.program_id(0)
-    nlat, nwave = 768, 512
-    lane = lax.broadcasted_iota(jnp.int32, (8, 128), 1)
-    left = lane < 64
-
-    @pl.when(r == 0)
+        rest(send_b, ch, recv_b, bs_sem, br_sem).wait_send()
+    for r in range(8):
+        pltpu.make_async_copy(spec32.at[r], prod_out.at[r], out_sem.at[r]).wait()
+
+
+def body_b(inc_ref, prod_ref, inc_out, prod_out):
+    @pl.when(pl.program_id(0) == 0)
     def _():
-        def put(s, v):
-            nat[pl.ds(pl.multiple_of(lat_ref[s] * 8, 8), 8), :] = v
-
-        for ch in range(NCH):
-
-            def open_up(e, c):
-                for p in range(2):
-                    s0 = e * 12 + ch * 4 + 2 * p
-                    t = back_ref[ch, e, :, p * 128 : (p + 1) * 128].astype(F32)
-                    lo, hi = t[0:8], t[8:16]
-                    put(s0, jnp.where(left, lo, pltpu.roll(hi, 64, 1)))
-                    put(s0 + 1, jnp.where(left, pltpu.roll(lo, 64, 1), hi))
-                return c
-
-            lax.fori_loop(0, 64, open_up, 0)
-
-    a = nat[pl.ds(r, nlat, stride=8), :].astype(BF16)
-    back = lax.dot_general(
-        a, table_ref[0], (((0,), (1,)), ((), ())), preferred_element_type=F32
-    )
-    acc[...] = back
-    keep = lax.broadcasted_iota(jnp.int32, (2, nwave), 1) < nwave - wave_ref[r]
+        inc_out[...] = inc_ref[...]
+
     for c in range(2):
-        for k in range(32):
-            out_ref[c, 0, k] = jnp.where(
-                keep, coef_ref[c, 0, k] + acc[pl.ds(c * 64 + 2 * k, 2), :], 0.0
-            )
+        prod_out[c, 0] = prod_ref[0, c * 64 : (c + 1) * 64].reshape(32, 2, 512)
 
 
 def body(coef, perturb, weight, table, wave_map, lat_map):
-    any_ = pl.BlockSpec(memory_space=pl.ANY)
+    wave_map, lat_map, coef, perturb, weight, table = [
+        pltpu.with_memory_space_constraint(v, pltpu.HBM)
+        for v in (wave_map, lat_map, coef, perturb, weight, table)
+    ]
+    hbm = pl.BlockSpec(memory_space=pltpu.HBM)
     smem = pl.BlockSpec(memory_space=pltpu.SMEM)
     dma = pltpu.SemaphoreType.DMA
-    inc, back = pl.pallas_call(
+    inc, product = pl.pallas_call(
         body_a,
         out_shape=(
             jax.ShapeDtypeStruct((12, 2, 1536), F32),
-            jax.ShapeDtypeStruct((NCH, 64, 16, 256), BF16),
+            jax.ShapeDtypeStruct((8, 128, 512), F32),
         ),
-        in_specs=[smem, smem, any_, any_, any_, any_],
-        out_specs=(pl.BlockSpec(memory_space=pltpu.VMEM), any_),
+        in_specs=[smem, smem, hbm, hbm, hbm, hbm],
+        out_specs=(pl.BlockSpec(memory_space=pltpu.VMEM), pl.BlockSpec(memory_space=pl.ANY)),
         scratch_shapes=[
             pltpu.VMEM((8, 512, 768), BF16),
             pltpu.VMEM((2, 8, 32, 2, 512), F32),
@@ -298,6 +347,9 @@
             pltpu.VMEM((24, 1536), F32),
             pltpu.VMEM((256, 1536), BF16),
             pltpu.VMEM((NCH, 64, 16, 256), BF16),
+            pltpu.VMEM((NCH, 64, 16, 256), BF16),
+            pltpu.VMEM((768, 768), BF16),
+            pltpu.VMEM((256, 8, 128), F32),
             dma((3,)),
             dma((8,)),
             dma((NCH,)),
@@ -307,31 +359,26 @@
             dma((NCH,)),
             dma((NCH,)),
             dma((2 * NCH,)),
-            dma,
+            dma((8,)),
         ],
         compiler_params=pltpu.CompilerParams(
-            collective_id=0, has_side_effects=True, vmem_limit_bytes=60 * 1024 * 1024
+            collective_id=0, has_side_effects=True, vmem_limit_bytes=44 * 1024 * 1024
         ),
         name="transforms",
     )(wave_map, lat_map, coef, perturb, weight, table)
-    own = lax.dynamic_slice_in_dim(wave_map, lax.axis_index("band") * 8, 8)
-    product = pl.pallas_call(
+    whole = pl.BlockSpec((12, 2, 1536), lambda r: (0, 0, 0))
+    return pl.pallas_call(
         body_b,
-        out_shape=jax.ShapeDtypeStruct((2, 8, 32, 2, 512), F32),
+        out_shape=(
+            jax.ShapeDtypeStruct((12, 2, 1536), F32),
+            jax.ShapeDtypeStruct((2, 8, 32, 2, 512), F32),
+        ),
         grid=(8,),
-        in_specs=[
-            smem,
-            smem,
-            pl.BlockSpec((NCH, 64, 16, 256), lambda r: (0, 0, 0, 0)),
-            pl.BlockSpec((1, 512, 768), lambda r: (r, 0, 0)),
-            pl.BlockSpec((2, 1, 32, 2, 512), lambda r: (0, r, 0, 0, 0)),
-        ],
-        out_specs=pl.BlockSpec((2, 1, 32, 2, 512), lambda r: (0, r, 0, 0, 0)),
-        scratch_shapes=[pltpu.VMEM((768 * 8, 128), F32), pltpu.VMEM((128, 512), F32)],
-        compiler_params=pltpu.CompilerParams(vmem_limit_bytes=60 * 1024 * 1024),
-        name="product",
-    )(own, lat_map, back, table, coef)
-    return inc, product
+        in_specs=[whole, pl.BlockSpec((1, 128, 512), lambda r: (r, 0, 0))],
+        out_specs=(whole, pl.BlockSpec((2, 1, 32, 2, 512), lambda r: (0, r, 0, 0, 0))),
+        compiler_params=pltpu.CompilerParams(vmem_limit_bytes=16 * 1024 * 1024),
+        name="place",
+    )(inc, product)
 
 
 def solution(mesh):

time: 121 us -> 90.9 us (0.75)
  Pallas kernels: 118 us -> 89.2 us
  local copies, waits for them, and re-layouts: 1.93 us -> 0 us
    pallas_call x1, Pallas kernels: 23.9 us -> 3.08 us  [body(): pl.pallas_call(body_b, out_shape=(jax.ShapeDtypeStruct((12, 2, 1536), F32...]
    pallas_call x1, Pallas kernels: 94.5 us -> 86.1 us  [body(): pl.pallas_call(body_a, out_shape=(jax.ShapeDtypeStruct((12, 2, 1536), F32...]
    dynamic_slice x1 -> x0, local copies, waits for them, and re-layouts: 1.27 us -> none  [body(): own = lax.dynamic_slice_in_dim(wave_map, lax.axis_index('band') * 8, 8)]
where the time goes in v1:
time: 90.9 us; the launch traced here: 89.8 us
  Pallas kernels  89.2 us (98%)
    pallas_call x1, Pallas kernels, body(): pl.pallas_call(body_a, out_shape=(jax.ShapeDtypeStruct((12, 2, 1536), F32...  86.1 us
    pallas_call x1, Pallas kernels, body(): pl.pallas_call(body_b, out_shape=(jax.ShapeDtypeStruct((12, 2, 1536), F32...  3.08 us

profile of v1, /device:TPU:1, one launch (start us, length us, event | category | flops | bytes accessed | tf_op | source)
XLA Modules:
  0.0 89.8 jit_solution(11328436738755977169)
XLA Ops:
  0.6 86.1 %transforms.1 = (f32[12,2,1536]{2,1,0:T(2,128)S(1)}, f32[8,128,512]{2,1,0:T(8,128)S(1)}) custom-call(s32[512]{0:T(512)} %wave_ref.1, s32[768]{0:T(1024)} %lat_ref.1, f32[2,8,32,2,512]{4,3,2,1,0:T(2,128)} %coef_hbm.1, bf16[12,32,2,1536]{3,2,1,0:T(2,128)(2,1)} %pert_hbm.1, f32[12,2,1536]{2,1,0:T(2,128)} %w_hbm.1, bf16[8,512,768]{2,1,0:T(8,128)(2,1)} %table_hbm.1), custom_call_target="tpu_custom_call" | custom-call | tf_op jit(solution)/shard_map/transforms/pallas_call | solution.py:324
  86.8 3.1 %place.1 = (f32[12,2,1536]{2,1,0:T(2,128)}, f32[2,8,32,2,512]{4,3,2,1,0:T(2,128)}) custom-call(f32[12,2,1536]{2,1,0:T(2,128)S(1)} %get-tuple-element.4.inc_ref, f32[8,128,512]{2,1,0:T(8,128)S(1)} %get-tuple-element.5.prod_ref), custom_call_target="tpu_custom_call" | custom-call | tf_op jit(solution)/shard_map/place/pallas_call | solution.py:370

commit v2 on v1

--- a/solution.py
+++ b/solution.py
@@ -19,7 +19,7 @@
     wave_ref, lat_ref, coef_hbm, pert_hbm, w_hbm, table_hbm,
     inc_out, prod_out,
     tab_v, coef_v, pert_v, w_v, spec32, nat, send_f, recv_f, xt, dft, pert32, w8, part, recv_i, inc_v, adj, send_b,
-    recv_b, pick, opened, in_sem, tab_sem, fs_sem, fr_sem, is_sem, ir_sem, bs_sem, br_sem, loc_sem, out_sem,
+    recv_b, pick, opened, held, in_sem, coef_sem, tab_sem, fs_sem, fr_sem, is_sem, ir_sem, bs_sem, br_sem, loc_sem,
 ):
     band = lax.axis_index("band")
     mem = lax.axis_index("mem")
@@ -29,24 +29,26 @@
     tcopies = [
         pltpu.make_async_copy(table_hbm.at[r], tab_v.at[r], tab_sem.at[r]) for r in range(8)
     ]
-    c_copy = pltpu.make_async_copy(coef_hbm, coef_v, in_sem.at[0])
+    ccopies = [
+        pltpu.make_async_copy(coef_hbm.at[:, r], coef_v.at[:, r], coef_sem.at[r]) for r in range(8)
+    ]
     p_copy = pltpu.make_async_copy(pert_hbm, pert_v, in_sem.at[1])
     w_copy = pltpu.make_async_copy(w_hbm, w_v, in_sem.at[2])
-    c_copy.start()
-    for t in tcopies:
-        t.start()
+    for r in range(8):
+        ccopies[r].start()
+        tcopies[r].start()
     p_copy.start()
     w_copy.start()
 
     barrier = pltpu.get_barrier_semaphore()
 
     def greet(i, c):
-        pl.semaphore_signal(
-            barrier, inc=1, device_id=(lax.rem(band + i, nb), mem), device_id_type=MESH
-        )
+        dz = 4 + jnp.where(i // 8 % 2 == 0, -(i // 16), i // 16 + 1)
+        e = lax.rem(band + dz * 8 + 7 - lax.rem(i, 8), nb)
+        pl.semaphore_signal(barrier, inc=1, device_id=(e, mem), device_id_type=MESH)
         return c
 
-    lax.fori_loop(1, nb, greet, 0)
+    lax.fori_loop(0, nb - 1, greet, 0)
     for i in range(1, nm):
         pl.semaphore_signal(
             barrier, inc=1, device_id=(band, lax.rem(mem + i, nm)), device_id_type=MESH
@@ -61,24 +63,30 @@
         dy, dx = b // 4, lax.rem(b, 4)
         return (lax.rem(z + dz, 8) * 2 + lax.rem(y + dy, 2)) * 4 + lax.rem(x + dx, 4)
 
-    c_copy.wait()
-    lane_j = lax.broadcasted_iota(jnp.int32, (2, nwave), 1)
-
-    def to_spec(r, c):
-        limit = nwave - wave_ref[band * 8 + r]
-        keep = lane_j < limit
-        for part_i in range(2):
-            for k in range(32):
-                v = coef_v[part_i, r, k]
-                spec32[r, pl.ds(part_i * 64 + 2 * k, 2), :] = jnp.where(keep, v, 0.0)
-        return c
-
-    lax.fori_loop(0, 8, to_spec, 0)
-
+    lane_j = lax.broadcasted_iota(jnp.int32, (64, nwave), 1)
+
+    def to_spec(r):
+        keep = lane_j < nwave - wave_ref[band * 8 + r]
+        for c in range(2):
+            spec32[r, c * 64 : (c + 1) * 64, :] = jnp.where(
+                keep, coef_v[c, r].reshape(64, nwave), 0.0
+            )
+
+    def turn(r):
+        nat.reshape(nlat * 8, 128)[pl.ds(r, nlat, stride=8), :] = held[r % 2].T
+
+    ccopies[0].wait()
+    to_spec(0)
     for r in range(8):
+        if r < 7:
+            ccopies[r + 1].wait()
         tcopies[r].wait()
-        f = jnp.dot(spec32[r].astype(BF16), tab_v[r], preferred_element_type=F32)
-        nat.reshape(nlat * 8, 128)[pl.ds(r, nlat, stride=8), :] = f.T
+        if r < 7:
+            to_spec(r + 1)
+        held[r % 2] = jnp.dot(spec32[r].astype(BF16), tab_v[r], preferred_element_type=F32)
+        if r > 0:
+            turn(r - 1)
+    turn(7)
 
     pl.semaphore_wait(barrier, nb - 1 + nm - 1)
 
@@ -289,8 +297,7 @@
                 spec32[r] += v
             else:
                 keep = lax.broadcasted_iota(jnp.int32, (128, nwave), 1) < nwave - wave_ref[band * 8 + r]
-                spec32[r] = jnp.where(keep, spec32[r] + v, 0.0)
-                pltpu.make_async_copy(spec32.at[r], prod_out.at[r], out_sem.at[r]).start()
+                prod_out[r] = jnp.where(keep, spec32[r] + v, 0.0)
 
     for ch in range(NCH):
         rest(send_f, ch, recv_f, fs_sem, fr_sem).wait_send()
@@ -300,8 +307,6 @@
                 device_id=(band, lax.rem(mem + i, nm)), device_id_type=MESH,
             ).wait_send()
         rest(send_b, ch, recv_b, bs_sem, br_sem).wait_send()
-    for r in range(8):
-        pltpu.make_async_copy(spec32.at[r], prod_out.at[r], out_sem.at[r]).wait()
 
 
 def body_b(inc_ref, prod_ref, inc_out, prod_out):
@@ -310,7 +315,8 @@
         inc_out[...] = inc_ref[...]
 
     for c in range(2):
-        prod_out[c, 0] = prod_ref[0, c * 64 : (c + 1) * 64].reshape(32, 2, 512)
+        for r in range(4):
+            prod_out[c, r] = prod_ref[r, c * 64 : (c + 1) * 64].reshape(32, 2, 512)
 
 
 def body(coef, perturb, weight, table, wave_map, lat_map):
@@ -328,7 +334,7 @@
             jax.ShapeDtypeStruct((8, 128, 512), F32),
         ),
         in_specs=[smem, smem, hbm, hbm, hbm, hbm],
-        out_specs=(pl.BlockSpec(memory_space=pltpu.VMEM), pl.BlockSpec(memory_space=pl.ANY)),
+        out_specs=(pl.BlockSpec(memory_space=pltpu.VMEM), pl.BlockSpec(memory_space=pltpu.VMEM)),
         scratch_shapes=[
             pltpu.VMEM((8, 512, 768), BF16),
             pltpu.VMEM((2, 8, 32, 2, 512), F32),
@@ -350,7 +356,9 @@
             pltpu.VMEM((NCH, 64, 16, 256), BF16),
             pltpu.VMEM((768, 768), BF16),
             pltpu.VMEM((256, 8, 128), F32),
+            pltpu.VMEM((2, 128, 768), F32),
             dma((3,)),
+            dma((8,)),
             dma((8,)),
             dma((NCH,)),
             dma((NCH,)),
@@ -359,7 +367,6 @@
             dma((NCH,)),
             dma((NCH,)),
             dma((2 * NCH,)),
-            dma((8,)),
         ],
         compiler_params=pltpu.CompilerParams(
             collective_id=0, has_side_effects=True, vmem_limit_bytes=44 * 1024 * 1024
@@ -373,9 +380,9 @@
             jax.ShapeDtypeStruct((12, 2, 1536), F32),
             jax.ShapeDtypeStruct((2, 8, 32, 2, 512), F32),
         ),
-        grid=(8,),
-        in_specs=[whole, pl.BlockSpec((1, 128, 512), lambda r: (r, 0, 0))],
-        out_specs=(whole, pl.BlockSpec((2, 1, 32, 2, 512), lambda r: (0, r, 0, 0, 0))),
+        grid=(2,),
+        in_specs=[whole, pl.BlockSpec((4, 128, 512), lambda r: (r, 0, 0))],
+        out_specs=(whole, pl.BlockSpec((2, 4, 32, 2, 512), lambda r: (0, r, 0, 0, 0))),
         compiler_params=pltpu.CompilerParams(vmem_limit_bytes=16 * 1024 * 1024),
         name="place",
     )(inc, product)

time: 90.9 us -> 88.2 us (0.970); the launches traced: 89.8 us -> 88.1 us
  Pallas kernels: 89.2 us -> 87.4 us
    pallas_call x1, Pallas kernels: 3.08 us -> 1.49 us  [body(): pl.pallas_call(body_b, out_shape=(jax.ShapeDtypeStruct((12, 2, 1536), F32...]
where the time goes in v2:
time: 88.2 us; the launch traced here: 88.1 us
  Pallas kernels  87.4 us (99%)
    pallas_call x1, Pallas kernels, body(): pl.pallas_call(body_a, out_shape=(jax.ShapeDtypeStruct((12, 2, 1536), F32...  86 us

profile of v2, /device:TPU:1, one launch (start us, length us, event | category | flops | bytes accessed | tf_op | source)
XLA Modules:
  0.0 88.1 jit_solution(7634126715383679880)
XLA Ops:
  0.6 86.0 %transforms.1 = (f32[12,2,1536]{2,1,0:T(2,128)S(1)}, f32[8,128,512]{2,1,0:T(8,128)S(1)}) custom-call(s32[512]{0:T(512)} %wave_ref.1, s32[768]{0:T(1024)} %lat_ref.1, f32[2,8,32,2,512]{4,3,2,1,0:T(2,128)} %coef_hbm.1, bf16[12,32,2,1536]{3,2,1,0:T(2,128)(2,1)} %pert_hbm.1, f32[12,2,1536]{2,1,0:T(2,128)} %w_hbm.1, bf16[8,512,768]{2,1,0:T(8,128)(2,1)} %table_hbm.1), custom_call_target="tpu_custom_call" | custom-call | tf_op jit(solution)/shard_map/transforms/pallas_call | solution.py:330
  86.6 1.5 %place.1 = (f32[12,2,1536]{2,1,0:T(2,128)}, f32[2,8,32,2,512]{4,3,2,1,0:T(2,128)}) custom-call(f32[12,2,1536]{2,1,0:T(2,128)S(1)} %get-tuple-element.4.inc_ref, f32[8,128,512]{2,1,0:T(8,128)S(1)} %get-tuple-element.5.prod_ref), custom_call_target="tpu_custom_call" | custom-call | tf_op jit(solution)/shard_map/place/pallas_call | solution.py:377

commit v3 on v2

--- a/solution.py
+++ b/solution.py
@@ -13,6 +13,8 @@
 BF16 = jnp.bfloat16
 
 NCH = 3
+STAGES = ((0, 0, 1), (1, 0, 1), (2, 0, 2), (2, 1, 2))
+NST = len(STAGES)
 
 
 def body_a(
@@ -93,22 +95,48 @@
     lane = lax.broadcasted_iota(jnp.int32, (8, 128), 1)
     left = lane < 64
 
-    def send_chunk(buf, ch, dst, s_sem, r_sem):
-        def one(i, c):
-            e = peer(i)
-            pltpu.make_async_remote_copy(
-                buf.at[ch, e], dst.at[ch, band], s_sem.at[ch], r_sem.at[ch],
-                device_id=(e, mem), device_id_type=MESH,
-            ).start()
-            return c
-
-        lax.fori_loop(0, nb - 1, one, 0)
-
     def rest(buf, ch, dst, s_sem, r_sem):
         return pltpu.make_async_remote_copy(
             buf.at[ch, pl.ds(0, nb - 1)], dst.at[ch, pl.ds(0, nb - 1)], s_sem.at[ch], r_sem.at[ch],
             device_id=(lax.rem(band + 1, nb), mem), device_id_type=MESH,
         )
+
+    def own_back(ch):
+        return pltpu.make_async_copy(
+            send_b.at[ch, band], recv_b.at[ch, band], loc_sem.at[NCH + ch]
+        )
+
+    def stage_of(st):
+        ch, half, halves = STAGES[st]
+        lo = half * 32
+        return ch, lo, nb - 1 if half == halves - 1 else 32
+
+    def send_back(st):
+        ch, lo, hi = stage_of(st)
+
+        def one(i, c):
+            e = peer(i)
+            pltpu.make_async_remote_copy(
+                send_b.at[ch, e], recv_b.at[ch, band], bs_sem.at[st], br_sem.at[st],
+                device_id=(e, mem), device_id_type=MESH,
+            ).start()
+            return c
+
+        lax.fori_loop(lo, hi, one, 0)
+
+    def rest_back(st):
+        ch, lo, hi = stage_of(st)
+        return pltpu.make_async_remote_copy(
+            send_b.at[ch, pl.ds(0, hi - lo)], recv_b.at[ch, pl.ds(0, hi - lo)],
+            bs_sem.at[st], br_sem.at[st],
+            device_id=(lax.rem(band + 1, nb), mem), device_id_type=MESH,
+        )
+
+    def source(st, n):
+        if STAGES[st][2] == 1:
+            return n
+        side = 1 - y if STAGES[st][1] == 0 else y
+        return n // 4 * 8 + side * 4 + n % 4
 
     def row(s):
         return nat[lat_ref[s]]
@@ -235,31 +263,38 @@
             return c
 
         lax.fori_loop(0, 4, back, 0)
-        pltpu.make_async_copy(
-            send_b.at[ch, band], recv_b.at[ch, band], loc_sem.at[NCH + ch]
-        ).start()
-        send_chunk(send_b, ch, recv_b, bs_sem, br_sem)
+        for st in range(NST):
+            if STAGES[st][0] == ch:
+                send_back(st)
+        own_back(ch).start()
 
     for s in range(12):
         inc_out[s] = inc_v[pl.ds(2 * s, 2), :]
 
-    def select(t, c):
-        halves = []
-        for h in range(2):
-            m = jnp.zeros((8, 128), jnp.int32)
-            for i in range(8):
-                k = h * 8 + i
-                m = jnp.where(row8 == i, lat_ref[(t % 16 * 4 + k // 4) * 12 + t // 16 * 4 + k % 4], m)
-            halves.append(m)
-        m = jnp.concatenate(halves, axis=0)
-        lane16 = lax.broadcasted_iota(jnp.int32, (16, 128), 1)
-        for b in range(nlat // 128):
-            pick[pl.ds(pl.multiple_of(t * 16, 16), 16), b * 128 : (b + 1) * 128] = jnp.where(
-                m == lane16 + b * 128, 1.0, 0.0
-            ).astype(BF16)
-        return c
-
-    lax.fori_loop(0, nlat // 16, select, 0, unroll=2)
+    lane16 = lax.broadcasted_iota(jnp.int32, (16, 128), 1)
+    first = 0
+    firsts = []
+    for st, (ch, _, halves_of) in enumerate(STAGES):
+        firsts.append(first)
+
+        def choose(t, c, st=st, ch=ch, first=first):
+            halves = []
+            for h in range(2):
+                m = jnp.zeros((8, 128), jnp.int32)
+                for i in range(8):
+                    k = h * 8 + i
+                    s = source(st, t * 4 + k // 4) * 12 + ch * 4 + k % 4
+                    m = jnp.where(row8 == i, lat_ref[s], m)
+                halves.append(m)
+            m = jnp.concatenate(halves, axis=0)
+            for b in range(nlat // 128):
+                pick[pl.ds(pl.multiple_of(first + t * 16, 16), 16), b * 128 : (b + 1) * 128] = (
+                    jnp.where(m == lane16 + b * 128, 1.0, 0.0).astype(BF16)
+                )
+            return c
+
+        lax.fori_loop(0, nb // 4 // halves_of, choose, 0, unroll=2)
+        first += nb * 4 // halves_of
 
     def arrange(r, c):
         tab_v[r] = lax.dot_general(
@@ -269,31 +304,32 @@
 
     lax.fori_loop(0, 8, arrange, 0)
 
-    for ch in range(NCH):
-        pltpu.make_async_copy(
-            send_b.at[ch, band], recv_b.at[ch, band], loc_sem.at[NCH + ch]
-        ).wait()
-        rest(send_b, ch, recv_b, bs_sem, br_sem).wait_recv()
-
-        def open_up(g, c):
+    for st, (ch, half, halves_of) in enumerate(STAGES):
+        if half == halves_of - 1:
+            own_back(ch).wait()
+        rest_back(st).wait_recv()
+        depth = nb * 4 // halves_of
+
+        def open_up(g, c, st=st, ch=ch):
             for k in range(8):
-                e = g * 8 + k
+                n = g * 8 + k
+                e = source(st, n)
                 for p in range(2):
                     t = recv_b[ch, e, :, p * 128 : (p + 1) * 128].astype(F32)
                     lo, hi = t[0:8], t[8:16]
-                    opened[e * 4 + 2 * p] = jnp.where(left, lo, pltpu.roll(hi, 64, 1))
-                    opened[e * 4 + 2 * p + 1] = jnp.where(left, pltpu.roll(lo, 64, 1), hi)
-            return c
-
-        lax.fori_loop(0, nb // 8, open_up, 0)
+                    opened[n * 4 + 2 * p] = jnp.where(left, lo, pltpu.roll(hi, 64, 1))
+                    opened[n * 4 + 2 * p + 1] = jnp.where(left, pltpu.roll(lo, 64, 1), hi)
+            return c
+
+        lax.fori_loop(0, nb // 8 // halves_of, open_up, 0)
 
         for r in range(8):
-            a = opened.reshape(2048, 128)[pl.ds(r, 256, stride=8), :].astype(BF16)
+            a = opened.reshape(2048, 128)[pl.ds(r, depth, stride=8), :].astype(BF16)
             v = lax.dot_general(
-                a, tab_v[r, :, ch * 256 : (ch + 1) * 256], (((0,), (1,)), ((), ())),
+                a, tab_v[r, :, firsts[st] : firsts[st] + depth], (((0,), (1,)), ((), ())),
                 preferred_element_type=F32,
             )
-            if ch < NCH - 1:
+            if st < NST - 1:
                 spec32[r] += v
             else:
                 keep = lax.broadcasted_iota(jnp.int32, (128, nwave), 1) < nwave - wave_ref[band * 8 + r]
@@ -306,7 +342,8 @@
                 part.at[ch], recv_i.at[ch, i - 1], is_sem.at[ch, i - 1], ir_sem.at[ch, i - 1],
                 device_id=(band, lax.rem(mem + i, nm)), device_id_type=MESH,
             ).wait_send()
-        rest(send_b, ch, recv_b, bs_sem, br_sem).wait_send()
+    for st in range(NST):
+        rest_back(st).wait_send()
 
 
 def body_b(inc_ref, prod_ref, inc_out, prod_out):
@@ -364,8 +401,8 @@
             dma((NCH,)),
             dma((NCH, 3)),
             dma((NCH, 3)),
-            dma((NCH,)),
-            dma((NCH,)),
+            dma((NST,)),
+            dma((NST,)),
             dma((2 * NCH,)),
         ],
         compiler_params=pltpu.CompilerParams(

time: 88.2 us -> 87.6 us (level)
  no operation moved by 1% of the time
where the time goes in v3:
time: 87.6 us; the launch traced here: 87.5 us
  Pallas kernels  86.9 us (99%)
    pallas_call x1, Pallas kernels, body(): pl.pallas_call(body_a, out_shape=(jax.ShapeDtypeStruct((12, 2, 1536), F32...  85.4 us

profile of v3, /device:TPU:1, one launch (start us, length us, event | category | flops | bytes accessed | tf_op | source)
XLA Modules:
  0.0 87.5 jit_solution(10001038933824278890)
XLA Ops:
  0.6 85.4 %transforms.1 = (f32[12,2,1536]{2,1,0:T(2,128)S(1)}, f32[8,128,512]{2,1,0:T(8,128)S(1)}) custom-call(s32[512]{0:T(512)} %wave_ref.1, s32[768]{0:T(1024)} %lat_ref.1, f32[2,8,32,2,512]{4,3,2,1,0:T(2,128)} %coef_hbm.1, bf16[12,32,2,1536]{3,2,1,0:T(2,128)(2,1)} %pert_hbm.1, f32[12,2,1536]{2,1,0:T(2,128)} %w_hbm.1, bf16[8,512,768]{2,1,0:T(8,128)(2,1)} %table_hbm.1), custom_call_target="tpu_custom_call" | custom-call | tf_op jit(solution)/shard_map/transforms/pallas_call | solution.py:367
  86.0 1.5 %place.1 = (f32[12,2,1536]{2,1,0:T(2,128)}, f32[2,8,32,2,512]{4,3,2,1,0:T(2,128)}) custom-call(f32[12,2,1536]{2,1,0:T(2,128)S(1)} %get-tuple-element.4.inc_ref, f32[8,128,512]{2,1,0:T(8,128)S(1)} %get-tuple-element.5.prod_ref), custom_call_target="tpu_custom_call" | custom-call | tf_op jit(solution)/shard_map/place/pallas_call | solution.py:414
